TPU v7x, 512 devices: a whole 4x8x8 slice. The times are simulated.
512 devices in a mesh: ctx: 64 (over z_lo, x, y), head: 8 (over z_hi, core).
Axes of the slice: x: 4, y: 8, z: 8 (z_hi: 4, z_lo: 2; z = z_hi * 2 + z_lo), core: 2. Of those that a mesh axis runs over, the one named last changes fastest.
Arguments:
- queries: bfloat16 [10240, 8192], P(('ctx', 'head')), may hold values from -18 to 18
- keys: bfloat16 [10240, 1024], P(('ctx', 'head')), may hold values from -4.5 to 4.5
- values: bfloat16 [10240, 1024], P(('ctx', 'head')), may hold values from -12 to 12
- block_order: int32 [128], replicated, may hold values from 0 to 127, each once
Outputs:
- attended: bfloat16 [10240, 8192], P(('ctx', 'head'))
Inputs may be any that keep to these rules, and one draw needn't show every extreme that they name: Storage block b holds sequence block block_order[b], its tokens in order; block_order is a permutation.
All inputs are finite; a program needn't handle non-finite values.
Results may differ from a plain program's by a relative error of at most 0.0049.
Values may be sent and summed in bfloat16 or wider, within the bound.
No kernel may reach another device: no remote copies, remote signals or barrier semaphores. Data moves between devices by JAX's collectives and lax.ppermute only.
A program may use at most 64 MiB of HBM per device.

v0:
```python
import math
import jax
import jax.numpy as jnp
import numpy as np
from jax import lax
from jax.sharding import PartitionSpec as P

QUERY_HEADS = 64
VALUE_KEY_HEADS = 8
HEAD_DIMENSION = 128


def token_positions(block_order, row_ids, block_rows):
    block_ids = row_ids // block_rows
    block_table = jnp.arange(block_order.shape[0], dtype=jnp.int32)
    chosen = jnp.sum(
        jnp.where(block_ids[:, None] == block_table[None, :], block_order[None, :], 0), axis=1
    )
    return chosen * block_rows + row_ids % block_rows


def attend(states, query_block, query_pos, key_rows, value_rows, key_pos, key_heads, score_scale):
    max_old, total_old, weighted_old = states
    query_count = query_block.shape[0]
    head_size = key_rows.shape[1] // key_heads
    heads_per_group = query_block.shape[1] // (key_heads * head_size)
    head_total = key_heads * heads_per_group
    query_split = query_block.reshape(query_count, key_heads, heads_per_group, head_size)
    key_split = key_rows.reshape(-1, key_heads, head_size)
    value_split = value_rows.reshape(-1, key_heads, head_size)
    scores = (
        jnp.einsum("qkgd,nkd->kgqn", query_split, key_split, preferred_element_type=jnp.float32)
        * score_scale
    )
    visible = key_pos[None, :] <= query_pos[:, None]
    scores = jnp.where(visible[None, None], scores, -jnp.inf)
    max_prev = max_old.reshape(key_heads, heads_per_group, query_count)
    max_new = jnp.maximum(max_prev, jnp.max(scores, axis=3))
    weights = jnp.exp(scores - max_new[..., None])
    rescale = jnp.exp(max_prev - max_new)
    total_new = total_old.reshape(key_heads, heads_per_group, query_count) * rescale + jnp.sum(
        weights, axis=3
    )
    mixed_values = jnp.einsum(
        "kgqn,nkd->qkgd",
        weights.astype(jnp.bfloat16),
        value_split,
        preferred_element_type=jnp.float32,
    )
    weighted_new = (
        weighted_old.reshape(query_count, key_heads, heads_per_group, head_size)
        * jnp.transpose(rescale, (2, 0, 1))[..., None]
        + mixed_values
    )
    return (
        max_new.reshape(head_total, query_count),
        total_new.reshape(head_total, query_count),
        weighted_new.reshape(query_count, head_total * head_size),
    )


def on_device(queries, keys, values, block_order):
    head_count = lax.axis_size("head")
    ctx_index = lax.axis_index("ctx")
    tokens_per_shard = queries.shape[0]
    query_heads = QUERY_HEADS // head_count
    heads_per_group = QUERY_HEADS // VALUE_KEY_HEADS
    local_kv = max(1, query_heads // heads_per_group)
    score_scale = HEAD_DIMENSION ** (-0.5)
    placement_index = np.array(
        [
            slot_number * query_heads // heads_per_group + offset
            for slot_number in range(head_count)
            for offset in range(local_kv)
        ],
        dtype=np.int32,
    )
    key_placements = keys.reshape(tokens_per_shard, VALUE_KEY_HEADS, HEAD_DIMENSION)[
        :, placement_index, :
    ].reshape(tokens_per_shard, head_count * local_kv * HEAD_DIMENSION)
    value_placements = values.reshape(tokens_per_shard, VALUE_KEY_HEADS, HEAD_DIMENSION)[
        :, placement_index, :
    ].reshape(tokens_per_shard, head_count * local_kv * HEAD_DIMENSION)
    tok_ctx = tokens_per_shard * head_count
    block_rows = tok_ctx // 2
    query_pos = token_positions(
        block_order, ctx_index * tok_ctx + jnp.arange(tok_ctx, dtype=jnp.int32), block_rows
    )

    def make_fold(query_all, key_heads, position_of):

        def tile(states, key_rows, value_rows, key_pos):
            updated = []
            for number in range(2):
                query_block = query_all[number * block_rows : (number + 1) * block_rows]
                block_pos = query_pos[number * block_rows : (number + 1) * block_rows]
                reach = jnp.min(key_pos) <= jnp.max(block_pos)
                updated.append(
                    lax.cond(
                        reach,
                        lambda carry_state: attend(
                            carry_state,
                            query_block,
                            block_pos,
                            key_rows,
                            value_rows,
                            key_pos,
                            key_heads,
                            score_scale,
                        ),
                        lambda carry_state: carry_state,
                        states[number],
                    )
                )
            return tuple(updated)

        def fold_step(states, key_piece, first_row):
            key_rows, value_rows = key_piece
            count = key_rows.shape[0]
            key_pos = position_of(jnp.arange(count, dtype=jnp.int32))
            piece_rows = tok_ctx * math.gcd(count // tok_ctx, 4)
            splits = count // piece_rows

            def scan_step(carry_states, parts):
                return (tile(carry_states, parts[0], parts[1], parts[2]), None)

            states, unused = lax.scan(
                scan_step,
                states,
                (
                    key_rows.reshape(splits, piece_rows, -1),
                    value_rows.reshape(splits, piece_rows, -1),
                    key_pos.reshape(splits, piece_rows),
                ),
            )
            return states

        return fold_step

    local_q, local_k, local_v = (
        lax.all_to_all(queries, "head", split_axis=1, concat_axis=0, tiled=True),
        lax.all_to_all(key_placements, "head", split_axis=1, concat_axis=0, tiled=True),
        lax.all_to_all(value_placements, "head", split_axis=1, concat_axis=0, tiled=True),
    )

    def full_positions(row_ids):
        return token_positions(block_order, row_ids, block_rows)

    fold_each = make_fold(local_q, local_kv, full_positions)
    one_state = (
        jnp.full((query_heads, block_rows), -1e30, jnp.float32),
        jnp.zeros((query_heads, block_rows), jnp.float32),
        jnp.zeros((block_rows, query_heads * HEAD_DIMENSION), jnp.float32),
    )
    states = fold_each(
        (one_state, one_state),
        (
            lax.all_gather(local_k, "ctx", axis=0, tiled=True),
            lax.all_gather(local_v, "ctx", axis=0, tiled=True),
        ),
        jnp.int32(0),
    )
    total_all = jnp.concatenate([states[0][1], states[1][1]], axis=1)
    weighted_all = jnp.concatenate([states[0][2], states[1][2]], axis=0)
    weighted_all = weighted_all.reshape(tok_ctx, query_heads, HEAD_DIMENSION)
    attended = (
        (weighted_all / total_all.T[:, :, None])
        .reshape(tok_ctx, query_heads * HEAD_DIMENSION)
        .astype(jnp.bfloat16)
    )
    return lax.all_to_all(attended, "head", split_axis=0, concat_axis=1, tiled=True)


def solution(mesh):
    placed = (P(("ctx", "head"), None), P(("ctx", "head"), None), P(("ctx", "head"), None), P())
    return jax.shard_map(
        on_device, mesh=mesh, in_specs=placed, out_specs=P(("ctx", "head"), None), check_vma=False
    )
```

profile of v0, /device:TPU:62, one launch (start us, length us, event | category | flops | bytes accessed | tf_op | source)
XLA Modules:
  0.0 792.8 jit_solution(8596616769344484240)
XLA Ops:
  6.5 0.8 copy.49
  8.0 18.4 %all_to_all.67 = bf16[20,8,128]{2,0,1:T(8,128)(2,1)S(1)} all-to-all(bf16[20,8,128]{2,0,1:T(8,128)(2,1)S(1)} %bitcast.142), channel_id=1, replica_groups=mesh['ctx'=64,'head'=8] {'head'}, dimensions={1} | all-to-all | bytes 81920 | tf_op jit(solution)/shard_map/all_to_all | solution.py:142
  27.0 0.8 copy.50
  28.4 10.5 %all_to_all.68 = bf16[20,8,128]{2,0,1:T(8,128)(2,1)S(1)} all-to-all(bf16[20,8,128]{2,0,1:T(8,128)(2,1)S(1)} %bitcast.141), channel_id=1, replica_groups=mesh['ctx'=64,'head'=8] {'head'}, dimensions={1} | all-to-all | bytes 81920 | tf_op jit(solution)/shard_map/all_to_all | solution.py:143
  39.6 1.2 copy.51
  40.8 0.9 copy.40
  41.8 3.5 all-to-all-start.2
  45.3 6.3 select_reduce_fusion
  51.8 0.8 slice_reduce_fusion
  52.7 7.9 all-to-all-done.2
  60.7 264.9 %all-gather.3.cloned.1.call-done = bf16[10240,128]{1,0:T(8,128)(2,1)} async-done(((bf16[160,128]{1,0:T(8,128)(2,1)}), bf16[10240,128]{1,0:T(8,128)(2,1)}) %all-gather.3.cloned.1.call-update) | async-done | bytes 2621456 | tf_op jit(solution)/shard_map/all_gather | solution.py:158
  325.5 302.4 %all-gather.5.cloned.1.call-done = bf16[10240,128]{1,0:T(8,128)(2,1)} async-done(((bf16[160,128]{1,0:T(8,128)(2,1)}), bf16[10240,128]{1,0:T(8,128)(2,1)}) %all-gather.5.cloned.1.call-update) | async-done | bytes 2621456 | tf_op jit(solution)/shard_map/all_gather | solution.py:159
  628.0 135.3 %while.21 = (s32[]{:T(128)}, f32[8,80]{1,0:T(8,128)S(1)}, f32[8,80]{1,0:T(8,128)S(1)}, f32[80,1024]{1,0:T(8,128)S(1)}, f32[8,80]{1,0:T(8,128)S(1)}, /*index=5*/f...) while((s32[]{:T(128)}, f32[8,80]{1,0:T(8,128)S(1)}, ...), condition=%wide.region_14.15_spmd, body=%wide.region_4.14_spmd.sunk | while | flops 425599360 | bytes 17010988 | solution.py:127
  628.0 0.6 dynamic-slice_reduce_fusion.3
  631.2 1.0 dynamic-slice_bitcast_fusion.3
  632.2 2.1 conditional.4
  634.3 2.1 conditional.5
  639.7 1.0 dynamic-slice_bitcast_fusion.3
  640.7 2.1 conditional.4
  642.8 2.1 conditional.5
  648.1 1.0 dynamic-slice_bitcast_fusion.3
  649.1 2.1 conditional.4
  651.2 2.1 conditional.5
  656.6 1.0 dynamic-slice_bitcast_fusion.3
  657.6 2.1 conditional.4
  659.7 2.1 conditional.5
  665.0 1.0 dynamic-slice_bitcast_fusion.3
  666.1 2.1 conditional.4
  668.1 2.1 conditional.5
  673.5 1.0 dynamic-slice_bitcast_fusion.3
  674.5 2.1 conditional.4
  676.6 2.1 conditional.5
  681.9 1.0 dynamic-slice_bitcast_fusion.3
  683.0 2.1 conditional.4
  685.0 2.1 conditional.5
  690.4 1.0 dynamic-slice_bitcast_fusion.3
  691.4 2.1 conditional.4
  693.5 2.1 conditional.5
  698.8 1.0 dynamic-slice_bitcast_fusion.3
  699.9 2.1 conditional.4
  701.9 2.1 conditional.5
  707.3 1.0 dynamic-slice_bitcast_fusion.3
  708.3 2.1 conditional.4
  710.4 2.1 conditional.5
  715.8 1.0 dynamic-slice_bitcast_fusion.3
  716.8 2.1 conditional.4
  718.9 2.1 conditional.5
  724.2 1.0 dynamic-slice_bitcast_fusion.3
  725.2 2.1 conditional.4
  727.3 2.1 conditional.5
  732.7 1.0 dynamic-slice_bitcast_fusion.3
  733.7 2.1 conditional.4
  735.8 2.1 conditional.5
  741.1 1.0 dynamic-slice_bitcast_fusion.3
  742.1 2.1 conditional.4
  744.2 2.1 conditional.5
  749.6 1.0 dynamic-slice_bitcast_fusion.3
  750.6 2.1 conditional.4
  752.7 2.1 conditional.5
  758.0 1.0 dynamic-slice_bitcast_fusion.3
  759.1 2.1 conditional.4
  761.1 2.1 conditional.5
  764.1 20.6 %all_to_all.69 = bf16[8,20,1024]{2,1,0:T(8,128)(2,1)S(1)} all-to-all(bf16[8,20,1024]{2,1,0:T(8,128)(2,1)S(1)} %divide_convert_fusion), channel_id=1, replica_groups=mesh['ctx'=64,'head'=8] {'head'}, dimensions={0} | all-to-all | bytes 655360 | tf_op jit(solution)/shard_map/all_to_all | solution.py:171
  784.9 1.0 copy.52
  (407 shorter events, 77.9 us)
Async XLA Ops:
  6.5 319.0 %all-gather.3.cloned.1.call-start = ((), (), s32[]{:S(2)}) async-start(), calls=%async_computation.4 | async-start | bytes 2662400 | tf_op jit(solution)/shard_map/all_gather | solution.py:158
  27.0 600.9 %all-gather.5.cloned.1.call-start = ((), (), s32[]{:S(2)}) async-start(), calls=%async_computation.5 | async-start | bytes 2662400 | tf_op jit(solution)/shard_map/all_gather | solution.py:159
  28.4 16.9 %copy-start = (s32[128]{0:T(128)S(1)}, s32[128]{0:T(128)}, u32[]{:S(2)}) copy-start(s32[128]{0:T(128)} %param.16) | copy-start | bytes 1540
  41.8 18.8 %all-to-all-start.2 = ((bf16[20,8,1024]{2,0,1:T(8,128)(2,1)}), bf16[20,8,1024]{2,0,1:T(8,128)(2,1)S(1)}, u32[]{:S(2)}, u32[]{:S(2)}) async-start(bf16[20,8,1024]{2,0,1:T(8,128)(2,1)} %copy.40), calls=%async_computation.2 | async-start | bytes 786432 | tf_op jit(solution)/shard_map/all_to_all | solution.py:141
Sparse Core Ops, SparseCore 0:
  27.1 298.3 all-gather.2
  327.6 300.2 all-gather.4
where the time goes:
time: 794 us; the launch traced here: 793 us
  waiting for transfers between devices  575 us (72%)
  blocking collectives  49.5 us (6%)
  loops' own time  44.3 us (6%)
  other arithmetic  40.1 us (5%)
  matrix products  33.5 us (4%)
  local copies, waits for them, and re-layouts  33.1 us (4%)
  between operations  13.6 us (2%)
    all_gather x1, waiting for transfers between devices, on_device(): lax.all_gather(local_v, 'ctx', axis=0, tiled=True)  302 us
    all_gather x1, waiting for transfers between devices, on_device(): lax.all_gather(local_k, 'ctx', axis=0, tiled=True)  265 us
    another operation x1, loops' own time, fold_step(): lax.scan(scan_step, states, (key_rows.reshape(splits, piece_rows, -1), va...  41.5 us
    all_to_all x1, blocking collectives, on_device(): lax.all_to_all(attended, 'head', split_axis=0, concat_axis=1, tiled=True)  20.6 us
    reduce_sum x32, other arithmetic, attend(): jnp.sum(weights, axis=3)  18.5 us
    all_to_all x1, blocking collectives, on_device(): lax.all_to_all(key_placements, 'head', split_axis=1, concat_axis=0, tiled...  18.4 us
    dot_general x32, matrix products, attend(): jnp.einsum('qkgd,nkd->kgqn', query_split, key_split, preferred_element_ty...  17.7 us
    squeeze x16, local copies, waits for them, and re-layouts, fold_step(): lax.scan(scan_step, states, (key_rows.reshape(splits, piece_rows, -1), va...  16.4 us
  transfers between devices with their start and end apart: 3, of which 3 were waited for; matrix products, arithmetic and copies ran while one was open for 1% of the time, Pallas kernels for 0%

commit v1 on v0

--- a/solution.py
+++ b/solution.py
@@ -155,7 +155,9 @@
     states = fold_each(
         (one_state, one_state),
         (
-            lax.all_gather(local_k, "ctx", axis=0, tiled=True),
+            jnp.concatenate(
+                lax.all_to_all(jnp.stack([local_k] * lax.axis_size("ctx")), "ctx", 0, 0), axis=0
+            ),
             lax.all_gather(local_v, "ctx", axis=0, tiled=True),
         ),
         jnp.int32(0),

time: 794 us -> 523 us (0.66)
  the two profiles are of different devices: /device:TPU:62 before, /device:TPU:1 now
where the time goes in v1:
time: 523 us; the launch traced here: 521 us
  waiting for transfers between devices  263 us (50%)
  blocking collectives  61.5 us (12%)
  loops' own time  45.4 us (9%)
  other arithmetic  39.1 us (7%)
  local copies, waits for them, and re-layouts  35.1 us (7%)
  starting transfers between devices  32.2 us (6%)
  matrix products  31.2 us (6%)
  between operations  13.6 us (3%)
    all_gather x1, waiting for transfers between devices, on_device(): lax.all_gather(local_v, 'ctx', axis=0, tiled=True)  241 us
    all_to_all x1, blocking collectives, on_device(): lax.all_to_all(attended, 'head', split_axis=0, concat_axis=1, tiled=True)  61.5 us
    another operation x1, loops' own time, fold_step(): lax.scan(scan_step, states, (key_rows.reshape(splits, piece_rows, -1), va...  42.7 us
    reduce_sum x30, other arithmetic, attend(): jnp.sum(weights, axis=3)  16.7 us
    dot_general x30, matrix products, attend(): jnp.einsum('qkgd,nkd->kgqn', query_split, key_split, preferred_element_ty...  16.6 us
    squeeze x16, local copies, waits for them, and re-layouts, fold_step(): lax.scan(scan_step, states, (key_rows.reshape(splits, piece_rows, -1), va...  16.4 us
    dot_general x30, matrix products, attend(): jnp.einsum('kgqn,nkd->qkgd', weights.astype(jnp.bfloat16), value_split, p...  14.6 us
    all_to_all x1, starting transfers between devices, on_device(): lax.all_to_all(jnp.stack([local_k] * lax.axis_size('ctx')), 'ctx', 0, 0)  12.3 us
  transfers between devices with their start and end apart: 5, of which 4 were waited for; matrix products, arithmetic and copies ran while one was open for 3% of the time, Pallas kernels for 0%

profile of v1, /device:TPU:1, one launch (start us, length us, event | category | flops | bytes accessed | tf_op | source)
XLA Modules:
  0.0 521.2 jit_solution(10992448271618052768)
XLA Ops:
  6.5 0.8 copy.48
  7.4 1.2 gather_fusion
  8.6 11.8 %all-to-all-start = ((bf16[20,8,128]{2,0,1:T(8,128)(2,1)}), bf16[20,8,128]{2,0,1:T(8,128)(2,1)S(1)}, u32[]{:S(2)}, u32[]{:S(2)}) async-start(bf16[20,8,128]{2,0,1:T(8,128)(2,1)} %bitcast.24), calls=%async_computation | async-start | bytes 98304 | tf_op jit(solution)/shard_map/all_to_all | solution.py:142
  21.2 1.2 gather_fusion.1
  22.4 5.5 %all-to-all-done = bf16[20,8,128]{2,0,1:T(8,128)(2,1)S(1)} async-done(((bf16[20,8,128]{2,0,1:T(8,128)(2,1)}), bf16[20,8,128]{2,0,1:T(8,128)(2,1)S(1)}, u32[]{:S(2)}, u32[]{:S(2)}) %all-to-all-start) | async-done | bytes 40992 | tf_op jit(solution)/shard_map/all_to_all | solution.py:142
  27.9 4.0 all-to-all-start.2
  31.9 1.2 copy.50
  33.1 0.9 copy.39
  34.1 5.2 all-to-all-done.2
  39.3 4.1 all-to-all-start.3
  44.1 11.2 %all-to-all-done.3 = bf16[20,8,1024]{2,0,1:T(8,128)(2,1)S(1)} async-done(((bf16[20,8,1024]{2,0,1:T(8,128)(2,1)}), bf16[20,8,1024]{2,0,1:T(8,128)(2,1)S(1)}, u32[]{:S(2)}, u32[]{:S(2)}) %all-to-all-start.3) | async-done | bytes 327712 | tf_op jit(solution)/shard_map/all_to_all | solution.py:141
  55.3 1.8 stack.5
  57.1 12.3 %all-to-all-start.1 = ((bf16[64,160,128]{2,1,0:T(8,128)(2,1)}), bf16[64,160,128]{2,1,0:T(8,128)(2,1)}, u32[]{:S(2)}, u32[]{:S(2)}) async-start(bf16[64,160,128]{2,1,0:T(8,128)(2,1)} %stack.5), calls=%async_computation.1 | async-start | bytes 5242880 | tf_op jit(solution)/shard_map/all_to_all | solution.py:159
  69.5 6.3 %select_reduce_fusion = s32[10240]{0:T(1024)S(1)} fusion(s32[128]{0:T(128)S(1)} %copy-done, s32[10240]{0:T(1024)S(1)} %add_select_fusion.1), kind=kLoop, calls=%fused_computation.44 | loop fusion | flops 3921920 | bytes 82432 | tf_op jit(solution)/shard_map/reduce_sum | solution.py:16
  76.9 241.1 %all-gather.2.cloned.1.call-done = bf16[10240,128]{1,0:T(8,128)(2,1)} async-done(((bf16[160,128]{1,0:T(8,128)(2,1)}), bf16[10240,128]{1,0:T(8,128)(2,1)}) %all-gather.2.cloned.1.call-update) | async-done | bytes 2621456 | tf_op jit(solution)/shard_map/all_gather | solution.py:161
  318.1 132.7 %while.21 = (s32[]{:T(128)}, f32[8,80]{1,0:T(8,128)S(1)}, f32[8,80]{1,0:T(8,128)S(1)}, f32[80,1024]{1,0:T(8,128)S(1)}, f32[8,80]{1,0:T(8,128)S(1)}, /*index=5*/f...) while((s32[]{:T(128)}, f32[8,80]{1,0:T(8,128)S(1)}, ...), condition=%wide.region_14.15_spmd, body=%wide.region_4.14_spmd.sunk | while | flops 425599360 | bytes 17010988 | solution.py:127
  321.5 1.0 dynamic-slice_bitcast_fusion.3
  322.5 2.0 conditional.4
  324.5 2.1 conditional.5
  330.0 1.0 dynamic-slice_bitcast_fusion.3
  331.0 2.0 conditional.4
  333.1 2.1 conditional.5
  338.6 1.0 dynamic-slice_bitcast_fusion.3
  339.6 2.0 conditional.4
  341.6 2.1 conditional.5
  347.1 1.0 dynamic-slice_bitcast_fusion.3
  348.1 2.0 conditional.4
  350.2 2.1 conditional.5
  355.7 1.0 dynamic-slice_bitcast_fusion.3
  356.7 2.1 conditional.5
  362.2 1.0 dynamic-slice_bitcast_fusion.3
  363.2 2.0 conditional.4
  365.3 2.1 conditional.5
  370.7 1.0 dynamic-slice_bitcast_fusion.3
  371.8 2.0 conditional.4
  373.8 2.1 conditional.5
  379.3 1.0 dynamic-slice_bitcast_fusion.3
  380.3 2.1 conditional.5
  385.8 1.0 dynamic-slice_bitcast_fusion.3
  386.8 2.0 conditional.4
  388.9 2.1 conditional.5
  394.3 1.0 dynamic-slice_bitcast_fusion.3
  395.4 2.0 conditional.4
  397.4 2.1 conditional.5
  402.9 1.0 dynamic-slice_bitcast_fusion.3
  403.9 2.0 conditional.4
  406.0 2.1 conditional.5
  411.4 1.0 dynamic-slice_bitcast_fusion.3
  412.5 2.0 conditional.4
  414.5 2.1 conditional.5
  420.0 1.0 dynamic-slice_bitcast_fusion.3
  421.0 2.0 conditional.4
  423.1 2.1 conditional.5
  428.5 1.0 dynamic-slice_bitcast_fusion.3
  429.6 2.0 conditional.4
  431.6 2.1 conditional.5
  437.1 1.0 dynamic-slice_bitcast_fusion.3
  438.1 2.0 conditional.4
  440.2 2.1 conditional.5
  445.6 1.0 dynamic-slice_bitcast_fusion.3
  446.7 2.0 conditional.4
  448.7 2.1 conditional.5
  451.6 61.5 %all_to_all.69 = bf16[8,20,1024]{2,1,0:T(8,128)(2,1)S(1)} all-to-all(bf16[8,20,1024]{2,1,0:T(8,128)(2,1)S(1)} %divide_convert_fusion), channel_id=1, replica_groups=mesh['ctx'=64,'head'=8] {'head'}, dimensions={0} | all-to-all | bytes 655360 | tf_op jit(solution)/shard_map/all_to_all | solution.py:173
  513.4 1.0 copy.51
  (387 shorter events, 74.7 us)
Async XLA Ops:
  8.6 19.3 %all-to-all-start = ((bf16[20,8,128]{2,0,1:T(8,128)(2,1)}), bf16[20,8,128]{2,0,1:T(8,128)(2,1)S(1)}, u32[]{:S(2)}, u32[]{:S(2)}) async-start(bf16[20,8,128]{2,0,1:T(8,128)(2,1)} %bitcast.24), calls=%async_computation | async-start | bytes 98304 | tf_op jit(solution)/shard_map/all_to_all | solution.py:142
  27.9 11.4 %all-to-all-start.2 = ((bf16[20,8,128]{2,0,1:T(8,128)(2,1)}), bf16[20,8,128]{2,0,1:T(8,128)(2,1)S(1)}, u32[]{:S(2)}, u32[]{:S(2)}) async-start(bf16[20,8,128]{2,0,1:T(8,128)(2,1)} %bitcast.27), calls=%async_computation.2 | async-start | bytes 98304 | tf_op jit(solution)/shard_map/all_to_all | solution.py:143
  39.3 16.0 %all-to-all-start.3 = ((bf16[20,8,1024]{2,0,1:T(8,128)(2,1)}), bf16[20,8,1024]{2,0,1:T(8,128)(2,1)S(1)}, u32[]{:S(2)}, u32[]{:S(2)}) async-start(bf16[20,8,1024]{2,0,1:T(8,128)(2,1)} %copy.39), calls=%async_computation.3 | async-start | bytes 786432 | tf_op jit(solution)/shard_map/all_to_all | solution.py:141
  43.4 274.6 %all-gather.2.cloned.1.call-start = ((), (), s32[]{:S(2)}) async-start(), calls=%async_computation.5 | async-start | bytes 2662400 | tf_op jit(solution)/shard_map/all_gather | solution.py:161
  57.1 12.3 %copy-start = (s32[128]{0:T(128)S(1)}, s32[128]{0:T(128)}, u32[]{:S(2)}) copy-start(s32[128]{0:T(128)} %param.16) | copy-start | bytes 1540
  57.1 260.9 %all-to-all-start.1 = ((bf16[64,160,128]{2,1,0:T(8,128)(2,1)}), bf16[64,160,128]{2,1,0:T(8,128)(2,1)}, u32[]{:S(2)}, u32[]{:S(2)}) async-start(bf16[64,160,128]{2,1,0:T(8,128)(2,1)} %stack.5), calls=%async_computation.1 | async-start | bytes 5242880 | tf_op jit(solution)/shard_map/all_to_all | solution.py:159
Sparse Core Ops, SparseCore 0:
  46.3 271.7 all-gather.1
